TPU v7x, 128 devices: a whole 4x4x4 slice. The times are simulated.
128 devices in a mesh: band: 8 (over y, z_hi), plane: 16 (over z_lo, x, core).
Axes of the slice: x: 4, y: 4, z: 4 (z_hi: 2, z_lo: 2; z = z_hi * 2 + z_lo), core: 2. Of those that a mesh axis runs over, the one named last changes fastest.
Arguments:
- orbitals: float32 [64, 96, 9216], P('band', 'plane'), may hold values from -6 to 6
Outputs:
- exchange_action: float32 [64, 96, 9216], P('band', 'plane')
All inputs are finite; a program needn't handle non-finite values.
Results may differ from a plain program's by a relative error of at most 0.0001.
Values sent between devices are 32-bit elements; how exact they have to be, the bound alone decides.
A program may use at most 128 MiB of HBM per device.

v0:
```python
import math
import jax
import jax.numpy as jnp
from jax import lax
from jax.sharding import PartitionSpec as P

PAIR = 2
ROUNDS = 4
OMEGA = 0.106
CELL = 41.05
ALPHA = 0.25
HIGHEST = lax.Precision.HIGHEST


def from_root(value, axis, source):
    kept = jnp.where(lax.axis_index(axis) == source, value, 0).astype(value.dtype)
    return lax.psum(kept, axis)


def hartley_table(count):
    index = jnp.arange(count, dtype=jnp.int32)
    product = index[:, None] * index[None, :] % count
    angle = product.astype(jnp.float32) * (2.0 * math.pi / count)
    return jnp.cos(angle) + jnp.sin(angle)


def frequencies(count):
    index = jnp.arange(count, dtype=jnp.int32)
    return jnp.where(index <= count // 2, index, index - count).astype(jnp.float32)


def screened_kernel(count, first, width):
    freq = frequencies(count)
    square = freq * freq
    middle = lax.dynamic_slice_in_dim(square, first, width)
    scale = (2.0 * math.pi / CELL) ** 2
    g_two = scale * (square[:, None, None] + middle[None, :, None] + square[None, None, :])
    positive = g_two > 0
    safe = jnp.where(positive, g_two, 1.0)
    value = 4.0 * math.pi / safe * -jnp.expm1(-safe / (4.0 * OMEGA * OMEGA))
    value = jnp.where(positive, value, math.pi / (OMEGA * OMEGA))
    return value / float(count**3)


def coulomb_solve(density, table, kernel):
    field = jnp.einsum("pxyz,zw->pxyw", density, table, precision=HIGHEST)
    field = jnp.einsum("pxyz,yv->pxvz", field, table, precision=HIGHEST)
    field = lax.all_to_all(field, "plane", split_axis=2, concat_axis=1, tiled=True)
    field = jnp.einsum("pxyz,xu->puyz", field, table, precision=HIGHEST) * kernel
    field = jnp.einsum("pxyz,xu->puyz", field, table, precision=HIGHEST)
    field = lax.all_to_all(field, "plane", split_axis=1, concat_axis=2, tiled=True)
    field = jnp.einsum("pxyz,zw->pxyw", field, table, precision=HIGHEST)
    return jnp.einsum("pxyz,yv->pxvz", field, table, precision=HIGHEST)


def fetch_pair(fields, turn):
    return from_root(fields[0:PAIR], "band", turn)


def local(orbitals):
    local_bands, planes, flat = orbitals.shape
    count = planes * lax.axis_size("plane")
    fields = orbitals.reshape(local_bands, planes, count, count)
    table = hartley_table(count)
    kernel = screened_kernel(count, lax.axis_index("plane") * planes, planes)
    shape_tail = (planes, count, count)
    local_sum = jnp.zeros_like(fields)
    owner_list = []
    for turn in range(ROUNDS):
        received = fetch_pair(fields, turn)
        density = (fields[:, None] * received[None]).reshape((local_bands * PAIR,) + shape_tail)
        potential = coulomb_solve(density, table, kernel).reshape((local_bands, PAIR) + shape_tail)
        local_sum = local_sum + jnp.sum(received[None] * potential, axis=1)
        owner_list.append(jnp.sum(fields[:, None] * potential, axis=0))
    owner_terms = jnp.stack(owner_list)
    own_extra = jnp.zeros((PAIR,) + shape_tail, jnp.float32)
    for turn in range(ROUNDS):
        summed = lax.psum(owner_terms[turn], "band")
        owner_flag = (lax.axis_index("band") == turn).astype(jnp.float32)
        own_extra = own_extra + owner_flag * summed
    local_sum = local_sum.at[0:PAIR].add(own_extra)
    return (-ALPHA * local_sum).reshape(local_bands, planes, count * count)


def solution(mesh):
    placed = (P("band", "plane", None),)
    return jax.shard_map(
        local, mesh=mesh, in_specs=placed, out_specs=P("band", "plane", None), check_vma=False
    )
```

profile of v0, /device:TPU:8, one launch (start us, length us, event | category | flops | bytes accessed | tf_op | source)
XLA Modules:
  0.0 886.8 jit_solution(3193934926200104955)
XLA Ops:
  16.1 122.7 %all-reduce.7.cloned.1.call-done = (f32[2,6,96,96]{3,2,0,1:T(8,128)}, f32[2,6,96,96]{3,2,0,1:T(8,128)}, f32[2,6,96,96]{3,2,0,1:T(8,128)}, f32[2,6,96,96]{3,2,0,1:T(8,128)}) async-done(((f32[2,6,96,96]{3,2,0,1:T(8,128)}, f32[2,6,96,96]{3,2,0,1:T(8,128)}, f32[2,6,96,96]{3,2,0,1:T(8,128)}, f32[2,6,96,96]{3,2,0,1:T(8,128)}), (f32[2,6,96,96]{3,2,0,1:T(8,128)}, f32[2,6,96,96]{3,2,0,1:T(8,128)}, ...) | async-done | bytes 1769488 | tf_op jit(solution)/shard_map/psum | solution.py:17
  138.8 9.3 %broadcast_multiply_fusion.2 = (f32[8,2,6,96,96]{4,3,2,1,0:T(8,128)}, f32[8,2,6,96,96]{4,3,2,1,0:T(8,128)}, f32[8,2,6,96,96]{4,3,2,1,0:T(8,128)}, f32[8,2,6,96,96]{4,3,2,1,0:T(8,128)}) fusion(f32[2,6,96,96]{3,2,0,1:T(8,128)} %get-tuple-element.27, f32[2,6,96,96]{3,2,0,1:T(8,128)} %get-tuple-element.26, f32[8,6,96,96]{3,2,0,1:T(8,128)S(1)} %mul.424, ...), kind=kLoop, calls=%fused_computation.39 | loop fusion | flops 3538944 | bytes 17694720 | tf_op jit(solution)/shard_map/mul | solution.py:71
  148.1 6.3 fusion.52
  158.9 4.9 copy.143
  163.8 4.8 all-to-all-start.4
  168.6 6.3 fusion.55
  179.5 4.9 copy.133
  184.4 47.5 %all-to-all-done.4 = f32[16,6,96,96]{3,0,1,2:T(8,128)} async-done(((f32[16,6,96,96]{3,0,1,2:T(8,128)}), f32[16,6,96,96]{3,0,1,2:T(8,128)}, u32[]{:S(2)}, u32[]{:S(2)}) %all-to-all-start.4) | async-done | bytes 3538976 | tf_op jit(solution)/shard_map/all_to_all | solution.py:48
  231.9 5.1 all-to-all-start.2
  237.1 6.3 fusion.49
  247.9 4.9 copy.153
  252.9 47.7 %all-to-all-done.2 = f32[16,6,96,96]{3,0,1,2:T(8,128)} async-done(((f32[16,6,96,96]{3,0,1,2:T(8,128)}), f32[16,6,96,96]{3,0,1,2:T(8,128)}, u32[]{:S(2)}, u32[]{:S(2)}) %all-to-all-start.2) | async-done | bytes 3538976 | tf_op jit(solution)/shard_map/all_to_all | solution.py:48
  300.6 4.7 all-to-all-start.6
  305.3 6.3 fusion.58
  316.2 4.9 copy.123
  321.1 47.7 %all-to-all-done.6 = f32[16,6,96,96]{3,0,1,2:T(8,128)} async-done(((f32[16,6,96,96]{3,0,1,2:T(8,128)}), f32[16,6,96,96]{3,0,1,2:T(8,128)}, u32[]{:S(2)}, u32[]{:S(2)}) %all-to-all-start.6) | async-done | bytes 3538976 | tf_op jit(solution)/shard_map/all_to_all | solution.py:48
  368.8 5.0 all-to-all-start
  377.1 7.1 fusion.14
  384.2 4.7 fusion.38
  389.0 4.9 copy.147
  393.9 42.9 %all-to-all-done = f32[16,6,96,96]{3,0,1,2:T(8,128)} async-done(((f32[16,6,96,96]{3,0,1,2:T(8,128)}), f32[16,6,96,96]{3,0,1,2:T(8,128)}, u32[]{:S(2)}, u32[]{:S(2)}) %all-to-all-start) | async-done | bytes 3538976 | tf_op jit(solution)/shard_map/all_to_all | solution.py:48
  436.8 4.6 all-to-all-start.5
  444.3 7.1 fusion.18
  451.5 5.0 fusion.35
  456.4 4.9 copy.137
  461.4 43.5 %all-to-all-done.5 = f32[16,96,6,96]{3,0,2,1:T(8,128)} async-done(((f32[16,96,6,96]{3,0,2,1:T(8,128)}), f32[16,96,6,96]{3,0,2,1:T(8,128)}, u32[]{:S(2)}, u32[]{:S(2)}) %all-to-all-start.5) | async-done | bytes 3538976 | tf_op jit(solution)/shard_map/all_to_all | solution.py:51
  504.9 4.6 all-to-all-start.3
  512.4 7.1 fusion.10
  519.5 4.7 fusion.41
  524.3 4.9 copy.157
  529.1 43.8 %all-to-all-done.3 = f32[16,96,6,96]{3,0,2,1:T(8,128)} async-done(((f32[16,96,6,96]{3,0,2,1:T(8,128)}), f32[16,96,6,96]{3,0,2,1:T(8,128)}, u32[]{:S(2)}, u32[]{:S(2)}) %all-to-all-start.3) | async-done | bytes 3538976 | tf_op jit(solution)/shard_map/all_to_all | solution.py:51
  572.9 4.6 all-to-all-start.7
  580.4 7.4 fusion.22
  587.8 5.3 fusion.32
  593.2 5.0 copy.127
  598.1 42.9 %all-to-all-done.7 = f32[16,96,6,96]{3,0,2,1:T(8,128)} async-done(((f32[16,96,6,96]{3,0,2,1:T(8,128)}), f32[16,96,6,96]{3,0,2,1:T(8,128)}, u32[]{:S(2)}, u32[]{:S(2)}) %all-to-all-start.7) | async-done | bytes 3538976 | tf_op jit(solution)/shard_map/all_to_all | solution.py:51
  658.8 7.0 fusion.12
  665.7 7.0 fusion.16
  672.7 7.0 fusion.8
  679.8 29.3 %all-to-all-done.1 = f32[16,96,6,96]{3,0,2,1:T(8,128)} async-done(((f32[16,96,6,96]{3,0,2,1:T(8,128)}), f32[16,96,6,96]{3,0,2,1:T(8,128)}, u32[]{:S(2)}, u32[]{:S(2)}) %all-to-all-start.1) | async-done | bytes 3538976 | tf_op jit(solution)/shard_map/all_to_all | solution.py:51
  711.9 5.4 fusion.20
  717.4 6.3 multiply_reduce_fusion.6
  723.7 6.6 multiply_reduce_fusion.5
  730.3 6.6 multiply_reduce_fusion.4
  736.9 6.8 multiply_reduce_fusion.7
  743.6 5.3 multiply_reduce_fusion.3
  748.9 4.8 add_add_fusion
  753.7 117.3 %all-reduce.5.cloned.1.call-done = (f32[2,6,96,96]{3,2,1,0:T(8,128)}, f32[2,6,96,96]{3,2,1,0:T(8,128)}, f32[2,6,96,96]{3,2,1,0:T(8,128)}, f32[2,6,96,96]{3,2,1,0:T(8,128)}) async-done(((f32[2,6,96,96]{3,2,1,0:T(8,128)}, f32[2,6,96,96]{3,2,1,0:T(8,128)}, f32[2,6,96,96]{3,2,1,0:T(8,128)}, f32[2,6,96,96]{3,2,1,0:T(8,128)}), (f32[2,6,96,96]{3,2,1,0:T(8,128)}, f32[2,6,96,96]{3,2,1,0:T(8,128)}, ...) | async-done | bytes 1769488 | tf_op jit(solution)/shard_map/psum | solution.py:78
  (60 shorter events, 68.8 us)
Async XLA Ops:
  6.5 132.2 %all-reduce.7.cloned.1.call-start = ((), (), s32[]{:S(2)}) async-start(), calls=%async_computation.9 | async-start | bytes 4718592 | tf_op jit(solution)/shard_map/psum | solution.py:17
  163.8 68.1 %all-to-all-start.4 = ((f32[16,6,96,96]{3,0,1,2:T(8,128)}), f32[16,6,96,96]{3,0,1,2:T(8,128)}, u32[]{:S(2)}, u32[]{:S(2)}) async-start(f32[16,6,96,96]{3,0,1,2:T(8,128)} %copy.143), calls=%async_computation.4 | async-start | bytes 9437184 | tf_op jit(solution)/shard_map/all_to_all | solution.py:48
  231.9 68.6 %all-to-all-start.2 = ((f32[16,6,96,96]{3,0,1,2:T(8,128)}), f32[16,6,96,96]{3,0,1,2:T(8,128)}, u32[]{:S(2)}, u32[]{:S(2)}) async-start(f32[16,6,96,96]{3,0,1,2:T(8,128)} %copy.133), calls=%async_computation.2 | async-start | bytes 9437184 | tf_op jit(solution)/shard_map/all_to_all | solution.py:48
  300.6 68.2 %all-to-all-start.6 = ((f32[16,6,96,96]{3,0,1,2:T(8,128)}), f32[16,6,96,96]{3,0,1,2:T(8,128)}, u32[]{:S(2)}, u32[]{:S(2)}) async-start(f32[16,6,96,96]{3,0,1,2:T(8,128)} %copy.153), calls=%async_computation.6 | async-start | bytes 9437184 | tf_op jit(solution)/shard_map/all_to_all | solution.py:48
  368.8 68.1 %all-to-all-start = ((f32[16,6,96,96]{3,0,1,2:T(8,128)}), f32[16,6,96,96]{3,0,1,2:T(8,128)}, u32[]{:S(2)}, u32[]{:S(2)}) async-start(f32[16,6,96,96]{3,0,1,2:T(8,128)} %copy.123), calls=%async_computation | async-start | bytes 9437184 | tf_op jit(solution)/shard_map/all_to_all | solution.py:48
  436.8 68.0 %all-to-all-start.5 = ((f32[16,96,6,96]{3,0,2,1:T(8,128)}), f32[16,96,6,96]{3,0,2,1:T(8,128)}, u32[]{:S(2)}, u32[]{:S(2)}) async-start(f32[16,96,6,96]{3,0,2,1:T(8,128)} %copy.147), calls=%async_computation.5 | async-start | bytes 9437184 | tf_op jit(solution)/shard_map/all_to_all | solution.py:51
  504.9 68.0 %all-to-all-start.3 = ((f32[16,96,6,96]{3,0,2,1:T(8,128)}), f32[16,96,6,96]{3,0,2,1:T(8,128)}, u32[]{:S(2)}, u32[]{:S(2)}) async-start(f32[16,96,6,96]{3,0,2,1:T(8,128)} %copy.137), calls=%async_computation.3 | async-start | bytes 9437184 | tf_op jit(solution)/shard_map/all_to_all | solution.py:51
  572.9 68.1 %all-to-all-start.7 = ((f32[16,96,6,96]{3,0,2,1:T(8,128)}), f32[16,96,6,96]{3,0,2,1:T(8,128)}, u32[]{:S(2)}, u32[]{:S(2)}) async-start(f32[16,96,6,96]{3,0,2,1:T(8,128)} %copy.157), calls=%async_computation.7 | async-start | bytes 9437184 | tf_op jit(solution)/shard_map/all_to_all | solution.py:51
  598.1 51.4 %copy-start.1 = (f32[2,6,96,96]{3,2,0,1:T(8,128)S(1)}, f32[2,6,96,96]{3,2,0,1:T(8,128)}, u32[]{:S(2)}) copy-start(f32[2,6,96,96]{3,2,0,1:T(8,128)} %get-tuple-element.27) | copy-start | bytes 1327108
  598.1 52.2 %copy-start = (f32[2,6,96,96]{3,2,0,1:T(8,128)S(1)}, f32[2,6,96,96]{3,2,0,1:T(8,128)}, u32[]{:S(2)}) copy-start(f32[2,6,96,96]{3,2,0,1:T(8,128)} %get-tuple-element.28) | copy-start | bytes 1327108
  641.1 68.0 %all-to-all-start.1 = ((f32[16,96,6,96]{3,0,2,1:T(8,128)}), f32[16,96,6,96]{3,0,2,1:T(8,128)}, u32[]{:S(2)}, u32[]{:S(2)}) async-start(f32[16,96,6,96]{3,0,2,1:T(8,128)} %copy.127), calls=%async_computation.1 | async-start | bytes 9437184 | tf_op jit(solution)/shard_map/all_to_all | solution.py:51
  645.6 225.4 %all-reduce.5.cloned.1.call-start = ((), (), s32[]{:S(2)}) async-start(), calls=%async_computation.8 | async-start | bytes 4718592 | tf_op jit(solution)/shard_map/psum | solution.py:78
  709.1 8.3 slice-start.4
  711.9 5.4 slice-start.5
  711.9 11.8 %slice-start.2 = ((s8[4718592]{0:T(1024)(128)(4,1)}), s8[4194304]{0:T(1024)(128)(4,1)S(1)}, s32[]{:S(2)}) async-start(s8[4718592]{0:T(1024)(128)(4,1)} %bitcast.181), calls=%async_computation.12 | async-start | bytes 8388608
  717.3 6.3 slice-start.3
  717.4 6.3 copy-start.4
  717.4 12.9 %slice-start = ((s8[4718592]{0:T(1024)(128)(4,1)}), s8[4194304]{0:T(1024)(128)(4,1)S(1)}, s32[]{:S(2)}) async-start(s8[4718592]{0:T(1024)(128)(4,1)} %bitcast.179), calls=%async_computation.10 | async-start | bytes 8388608
  723.7 6.6 slice-start.1
  723.7 6.6 copy-start.3
  730.3 6.6 copy-start.2
Sparse Core Ops, SparseCore 0:
  13.8 124.9 all-reduce.6
  749.0 121.9 all-reduce.4
where the time goes:
time: 890 us; the launch traced here: 887 us
  waiting for transfers between devices  585 us (66%)
  matrix products  144 us (16%)
  local copies, waits for them, and re-layouts  79.6 us (9%)
  starting transfers between devices  37.9 us (4%)
  other arithmetic  25.4 us (3%)
  between operations  14.1 us (2%)
    all_to_all x4, waiting for transfers between devices, coulomb_solve(): lax.all_to_all(field, 'plane', split_axis=2, concat_axis=1, tiled=True)  186 us
    all_to_all x4, waiting for transfers between devices, coulomb_solve(): lax.all_to_all(field, 'plane', split_axis=1, concat_axis=2, tiled=True)  160 us
    psum x1, waiting for transfers between devices, from_root(): return lax.psum(kept, axis)  123 us
    psum x1, waiting for transfers between devices, local(): summed = lax.psum(owner_terms[turn], 'band')  117 us
    dot_general x4, matrix products, coulomb_solve(): jnp.einsum('pxyz,xu->puyz', field, table, precision=HIGHEST) * kernel  28.7 us
    dot_general x4, matrix products, coulomb_solve(): field = jnp.einsum('pxyz,zw->pxyw', field, table, precision=HIGHEST)  26.4 us
    dot_general x4, matrix products, coulomb_solve(): return jnp.einsum('pxyz,yv->pxvz', field, table, precision=HIGHEST)  26.2 us
    dot_general x4, matrix products, coulomb_solve(): field = jnp.einsum('pxyz,zw->pxyw', density, table, precision=HIGHEST)  25.4 us
  transfers between devices with their start and end apart: 10, of which 10 were waited for; matrix products, arithmetic and copies ran while one was open for 19% of the time, Pallas kernels for 0%

commit v1 on v0

--- a/solution.py
+++ b/solution.py
@@ -75,7 +75,9 @@
     owner_terms = jnp.stack(owner_list)
     own_extra = jnp.zeros((PAIR,) + shape_tail, jnp.float32)
     for turn in range(ROUNDS):
-        summed = lax.psum(owner_terms[turn], "band")
+        x = owner_terms[turn]
+        shards = lax.all_gather(x, "band", axis=0, tiled=False)
+        summed = shards.sum(axis=0)
         owner_flag = (lax.axis_index("band") == turn).astype(jnp.float32)
         own_extra = own_extra + owner_flag * summed
     local_sum = local_sum.at[0:PAIR].add(own_extra)

time: 890 us -> 1080 us (1.21)
  waiting for transfers between devices: 585 us -> 755 us
  other arithmetic: 25.4 us -> 38.4 us
    all_gather x0 -> x4, waiting for transfers between devices: none -> 286 us  [local(): shards = lax.all_gather(x, 'band', axis=0, tiled=False)]
    psum x1 -> x0, waiting for transfers between devices: 117 us -> none  [local(): summed = lax.psum(owner_terms[turn], 'band')]
    reduce_sum x0 -> x4, other arithmetic: none -> 13.3 us  [local(): summed = shards.sum(axis=0)]
  transfers between devices with their start and end apart: 10 -> 13, of which waited for: 10 -> 13; matrix products, arithmetic and copies ran while one was open for 19% -> 17% of each run, Pallas kernels for 0% -> 0%
where the time goes in v1:
time: 1080 us; the launch traced here: 1070 us
  waiting for transfers between devices  755 us (70%)
  matrix products  144 us (13%)
  local copies, waits for them, and re-layouts  79.8 us (7%)
  other arithmetic  38.4 us (4%)
  starting transfers between devices  38.2 us (4%)
  between operations  14 us (1%)
    all_gather x4, waiting for transfers between devices, local(): shards = lax.all_gather(x, 'band', axis=0, tiled=False)  286 us
    all_to_all x4, waiting for transfers between devices, coulomb_solve(): lax.all_to_all(field, 'plane', split_axis=2, concat_axis=1, tiled=True)  186 us
    all_to_all x4, waiting for transfers between devices, coulomb_solve(): lax.all_to_all(field, 'plane', split_axis=1, concat_axis=2, tiled=True)  160 us
    psum x1, waiting for transfers between devices, from_root(): return lax.psum(kept, axis)  123 us
    dot_general x4, matrix products, coulomb_solve(): jnp.einsum('pxyz,xu->puyz', field, table, precision=HIGHEST) * kernel  28.7 us
    dot_general x4, matrix products, coulomb_solve(): field = jnp.einsum('pxyz,zw->pxyw', field, table, precision=HIGHEST)  26.2 us
    dot_general x4, matrix products, coulomb_solve(): return jnp.einsum('pxyz,yv->pxvz', field, table, precision=HIGHEST)  26.2 us
    dot_general x4, matrix products, coulomb_solve(): field = jnp.einsum('pxyz,zw->pxyw', density, table, precision=HIGHEST)  25.4 us
  transfers between devices with their start and end apart: 13, of which 13 were waited for; matrix products, arithmetic and copies ran while one was open for 17% of the time, Pallas kernels for 0%

profile of v1, /device:TPU:8, one launch (start us, length us, event | category | flops | bytes accessed | tf_op | source)
XLA Modules:
  0.0 1070.1 jit_solution(8239067504499139061)
XLA Ops:
  16.1 122.6 %all-reduce.3.cloned.1.call-done = (f32[2,6,96,96]{3,2,0,1:T(8,128)}, f32[2,6,96,96]{3,2,0,1:T(8,128)}, f32[2,6,96,96]{3,2,0,1:T(8,128)}, f32[2,6,96,96]{3,2,0,1:T(8,128)}) async-done(((f32[2,6,96,96]{3,2,0,1:T(8,128)}, f32[2,6,96,96]{3,2,0,1:T(8,128)}, f32[2,6,96,96]{3,2,0,1:T(8,128)}, f32[2,6,96,96]{3,2,0,1:T(8,128)}), (f32[2,6,96,96]{3,2,0,1:T(8,128)}, f32[2,6,96,96]{3,2,0,1:T(8,128)}, ...) | async-done | bytes 1769488 | tf_op jit(solution)/shard_map/psum | solution.py:17
  138.8 9.3 broadcast_multiply_fusion.2
  148.1 6.3 fusion.52
  158.9 4.9 copy.143
  163.8 4.8 all-to-all-start.4
  168.7 6.3 fusion.55
  179.5 5.0 copy.133
  184.5 47.5 %all-to-all-done.4 = f32[16,6,96,96]{3,0,1,2:T(8,128)} async-done(((f32[16,6,96,96]{3,0,1,2:T(8,128)}), f32[16,6,96,96]{3,0,1,2:T(8,128)}, u32[]{:S(2)}, u32[]{:S(2)}) %all-to-all-start.4) | async-done | bytes 3538976 | tf_op jit(solution)/shard_map/all_to_all | solution.py:48
  232.0 5.2 all-to-all-start.2
  237.2 6.3 fusion.49
  248.0 4.9 copy.153
  253.0 47.7 %all-to-all-done.2 = f32[16,6,96,96]{3,0,1,2:T(8,128)} async-done(((f32[16,6,96,96]{3,0,1,2:T(8,128)}), f32[16,6,96,96]{3,0,1,2:T(8,128)}, u32[]{:S(2)}, u32[]{:S(2)}) %all-to-all-start.2) | async-done | bytes 3538976 | tf_op jit(solution)/shard_map/all_to_all | solution.py:48
  300.7 4.7 all-to-all-start.6
  305.4 6.3 fusion.58
  316.3 5.0 copy.123
  321.2 47.7 %all-to-all-done.6 = f32[16,6,96,96]{3,0,1,2:T(8,128)} async-done(((f32[16,6,96,96]{3,0,1,2:T(8,128)}), f32[16,6,96,96]{3,0,1,2:T(8,128)}, u32[]{:S(2)}, u32[]{:S(2)}) %all-to-all-start.6) | async-done | bytes 3538976 | tf_op jit(solution)/shard_map/all_to_all | solution.py:48
  368.9 5.0 all-to-all-start
  377.2 7.1 fusion.14
  384.3 4.7 fusion.38
  389.1 4.9 copy.147
  394.0 42.9 %all-to-all-done = f32[16,6,96,96]{3,0,1,2:T(8,128)} async-done(((f32[16,6,96,96]{3,0,1,2:T(8,128)}), f32[16,6,96,96]{3,0,1,2:T(8,128)}, u32[]{:S(2)}, u32[]{:S(2)}) %all-to-all-start) | async-done | bytes 3538976 | tf_op jit(solution)/shard_map/all_to_all | solution.py:48
  444.4 7.1 fusion.18
  451.6 5.0 fusion.35
  456.5 5.0 copy.137
  461.5 43.5 %all-to-all-done.5 = f32[16,96,6,96]{3,0,2,1:T(8,128)} async-done(((f32[16,96,6,96]{3,0,2,1:T(8,128)}), f32[16,96,6,96]{3,0,2,1:T(8,128)}, u32[]{:S(2)}, u32[]{:S(2)}) %all-to-all-start.5) | async-done | bytes 3538976 | tf_op jit(solution)/shard_map/all_to_all | solution.py:51
  512.5 7.1 fusion.10
  519.6 4.7 fusion.41
  524.4 4.9 copy.157
  529.2 43.8 %all-to-all-done.3 = f32[16,96,6,96]{3,0,2,1:T(8,128)} async-done(((f32[16,96,6,96]{3,0,2,1:T(8,128)}), f32[16,96,6,96]{3,0,2,1:T(8,128)}, u32[]{:S(2)}, u32[]{:S(2)}) %all-to-all-start.3) | async-done | bytes 3538976 | tf_op jit(solution)/shard_map/all_to_all | solution.py:51
  580.6 7.4 fusion.22
  588.0 5.3 fusion.32
  593.3 5.0 copy.127
  598.3 42.9 %all-to-all-done.7 = f32[16,96,6,96]{3,0,2,1:T(8,128)} async-done(((f32[16,96,6,96]{3,0,2,1:T(8,128)}), f32[16,96,6,96]{3,0,2,1:T(8,128)}, u32[]{:S(2)}, u32[]{:S(2)}) %all-to-all-start.7) | async-done | bytes 3538976 | tf_op jit(solution)/shard_map/all_to_all | solution.py:51
  658.9 6.9 fusion.12
  665.8 6.9 fusion.16
  672.7 7.1 fusion.8
  679.8 29.5 %all-to-all-done.1 = f32[16,96,6,96]{3,0,2,1:T(8,128)} async-done(((f32[16,96,6,96]{3,0,2,1:T(8,128)}), f32[16,96,6,96]{3,0,2,1:T(8,128)}, u32[]{:S(2)}, u32[]{:S(2)}) %all-to-all-start.1) | async-done | bytes 3538976 | tf_op jit(solution)/shard_map/all_to_all | solution.py:51
  712.2 5.4 fusion.20
  717.6 6.3 multiply_reduce_fusion.6
  724.0 6.5 multiply_reduce_fusion.5
  730.6 6.5 multiply_reduce_fusion.4
  737.1 6.8 multiply_reduce_fusion.7
  743.9 5.2 multiply_reduce_fusion.3
  751.1 4.9 add_add_fusion
  756.0 67.3 %all-gather.9.cloned.1.call-done = f32[16,6,96,96]{3,2,1,0:T(8,128)} async-done(((f32[2,6,96,96]{3,2,1,0:T(8,128)}), f32[16,6,96,96]{3,2,1,0:T(8,128)}) %all-gather.9.cloned.1.call-update) | async-done | bytes 3538960 | tf_op jit(solution)/shard_map/all_gather | solution.py:79
  826.2 73.1 %all-gather.11.cloned.1.call-done = f32[16,6,96,96]{3,2,1,0:T(8,128)} async-done(((f32[2,6,96,96]{3,2,1,0:T(8,128)}), f32[16,6,96,96]{3,2,1,0:T(8,128)}) %all-gather.11.cloned.1.call-update) | async-done | bytes 3538960 | tf_op jit(solution)/shard_map/all_gather | solution.py:79
  902.3 73.0 %all-gather.13.cloned.1.call-done = f32[16,6,96,96]{3,2,1,0:T(8,128)} async-done(((f32[2,6,96,96]{3,2,1,0:T(8,128)}), f32[16,6,96,96]{3,2,1,0:T(8,128)}) %all-gather.13.cloned.1.call-update) | async-done | bytes 3538960 | tf_op jit(solution)/shard_map/all_gather | solution.py:79
  979.0 72.1 %all-gather.15.cloned.1.call-done = f32[16,6,96,96]{3,2,1,0:T(8,128)} async-done(((f32[2,6,96,96]{3,2,1,0:T(8,128)}), f32[16,6,96,96]{3,2,1,0:T(8,128)}) %all-gather.15.cloned.1.call-update) | async-done | bytes 3538960 | tf_op jit(solution)/shard_map/all_gather | solution.py:79
  (73 shorter events, 97.5 us)
Async XLA Ops:
  6.5 132.2 %all-reduce.3.cloned.1.call-start = ((), (), s32[]{:S(2)}) async-start(), calls=%async_computation.12 | async-start | bytes 4718592 | tf_op jit(solution)/shard_map/psum | solution.py:17
  163.8 68.1 %all-to-all-start.4 = ((f32[16,6,96,96]{3,0,1,2:T(8,128)}), f32[16,6,96,96]{3,0,1,2:T(8,128)}, u32[]{:S(2)}, u32[]{:S(2)}) async-start(f32[16,6,96,96]{3,0,1,2:T(8,128)} %copy.143), calls=%async_computation.4 | async-start | bytes 9437184 | tf_op jit(solution)/shard_map/all_to_all | solution.py:48
  232.0 68.7 %all-to-all-start.2 = ((f32[16,6,96,96]{3,0,1,2:T(8,128)}), f32[16,6,96,96]{3,0,1,2:T(8,128)}, u32[]{:S(2)}, u32[]{:S(2)}) async-start(f32[16,6,96,96]{3,0,1,2:T(8,128)} %copy.133), calls=%async_computation.2 | async-start | bytes 9437184 | tf_op jit(solution)/shard_map/all_to_all | solution.py:48
  300.7 68.2 %all-to-all-start.6 = ((f32[16,6,96,96]{3,0,1,2:T(8,128)}), f32[16,6,96,96]{3,0,1,2:T(8,128)}, u32[]{:S(2)}, u32[]{:S(2)}) async-start(f32[16,6,96,96]{3,0,1,2:T(8,128)} %copy.153), calls=%async_computation.6 | async-start | bytes 9437184 | tf_op jit(solution)/shard_map/all_to_all | solution.py:48
  368.9 68.1 %all-to-all-start = ((f32[16,6,96,96]{3,0,1,2:T(8,128)}), f32[16,6,96,96]{3,0,1,2:T(8,128)}, u32[]{:S(2)}, u32[]{:S(2)}) async-start(f32[16,6,96,96]{3,0,1,2:T(8,128)} %copy.123), calls=%async_computation | async-start | bytes 9437184 | tf_op jit(solution)/shard_map/all_to_all | solution.py:48
  436.9 68.1 %all-to-all-start.5 = ((f32[16,96,6,96]{3,0,2,1:T(8,128)}), f32[16,96,6,96]{3,0,2,1:T(8,128)}, u32[]{:S(2)}, u32[]{:S(2)}) async-start(f32[16,96,6,96]{3,0,2,1:T(8,128)} %copy.147), calls=%async_computation.5 | async-start | bytes 9437184 | tf_op jit(solution)/shard_map/all_to_all | solution.py:51
  505.0 68.0 %all-to-all-start.3 = ((f32[16,96,6,96]{3,0,2,1:T(8,128)}), f32[16,96,6,96]{3,0,2,1:T(8,128)}, u32[]{:S(2)}, u32[]{:S(2)}) async-start(f32[16,96,6,96]{3,0,2,1:T(8,128)} %copy.137), calls=%async_computation.3 | async-start | bytes 9437184 | tf_op jit(solution)/shard_map/all_to_all | solution.py:51
  573.0 68.1 %all-to-all-start.7 = ((f32[16,96,6,96]{3,0,2,1:T(8,128)}), f32[16,96,6,96]{3,0,2,1:T(8,128)}, u32[]{:S(2)}, u32[]{:S(2)}) async-start(f32[16,96,6,96]{3,0,2,1:T(8,128)} %copy.157), calls=%async_computation.7 | async-start | bytes 9437184 | tf_op jit(solution)/shard_map/all_to_all | solution.py:51
  598.2 51.4 %copy-start.1 = (f32[2,6,96,96]{3,2,0,1:T(8,128)S(1)}, f32[2,6,96,96]{3,2,0,1:T(8,128)}, u32[]{:S(2)}) copy-start(f32[2,6,96,96]{3,2,0,1:T(8,128)} %get-tuple-element.23) | copy-start | bytes 1327108
  598.2 52.2 %copy-start = (f32[2,6,96,96]{3,2,0,1:T(8,128)S(1)}, f32[2,6,96,96]{3,2,0,1:T(8,128)}, u32[]{:S(2)}) copy-start(f32[2,6,96,96]{3,2,0,1:T(8,128)} %get-tuple-element.24) | copy-start | bytes 1327108
  641.2 68.1 %all-to-all-start.1 = ((f32[16,96,6,96]{3,0,2,1:T(8,128)}), f32[16,96,6,96]{3,0,2,1:T(8,128)}, u32[]{:S(2)}, u32[]{:S(2)}) async-start(f32[16,96,6,96]{3,0,2,1:T(8,128)} %copy.127), calls=%async_computation.1 | async-start | bytes 9437184 | tf_op jit(solution)/shard_map/all_to_all | solution.py:51
  645.7 177.6 %all-gather.9.cloned.1.call-start = ((), (), s32[]{:S(2)}) async-start(), calls=%async_computation.8 | async-start | bytes 5308416 | tf_op jit(solution)/shard_map/all_gather | solution.py:79
  709.2 8.4 slice-start.4
  712.2 5.4 slice-start.5
  712.2 11.8 %slice-start.2 = ((s8[4718592]{0:T(1024)(128)(4,1)}), s8[4194304]{0:T(1024)(128)(4,1)S(1)}, s32[]{:S(2)}) async-start(s8[4718592]{0:T(1024)(128)(4,1)} %bitcast.185), calls=%async_computation.15 | async-start | bytes 8388608
  717.6 6.4 slice-start.3
  717.6 6.3 copy-start.4
  717.6 12.9 %slice-start = ((s8[4718592]{0:T(1024)(128)(4,1)}), s8[4194304]{0:T(1024)(128)(4,1)S(1)}, s32[]{:S(2)}) async-start(s8[4718592]{0:T(1024)(128)(4,1)} %bitcast.183), calls=%async_computation.13 | async-start | bytes 8388608
  724.0 6.6 slice-start.1
  724.0 6.6 copy-start.3
  730.6 6.6 copy-start.2
  749.1 150.2 %all-gather.11.cloned.1.call-start = ((), (), s32[]{:S(2)}) async-start(), calls=%async_computation.9 | async-start | bytes 5308416 | tf_op jit(solution)/shard_map/all_gather | solution.py:79
  749.9 225.4 %all-gather.13.cloned.1.call-start = ((), (), s32[]{:S(2)}) async-start(), calls=%async_computation.10 | async-start | bytes 5308416 | tf_op jit(solution)/shard_map/all_gather | solution.py:79
  750.4 300.7 %all-gather.15.cloned.1.call-start = ((), (), s32[]{:S(2)}) async-start(), calls=%async_computation.11 | async-start | bytes 5308416 | tf_op jit(solution)/shard_map/all_gather | solution.py:79
Sparse Core Ops, SparseCore 0:
  13.8 124.9 all-reduce.2
  749.2 74.0 all-gather.8
  825.6 73.6 all-gather.10
  901.5 73.6 all-gather.12
  977.4 73.6 all-gather.14
